TPU v7x, 32 devices: a whole 2x2x4 slice. The times are simulated.
32 devices in a mesh: shot: 8 (over y, x, core), rcv: 4 (over z).
Axes of the slice: x: 2, y: 2, z: 4, core: 2. Of those that a mesh axis runs over, the one named last changes fastest.
Arguments:
- traces: bfloat16 [256, 512, 256], P('shot', 'rcv'), may hold values from -6 to 6
- shift_index: int32 [256, 512], P('shot', 'rcv'), may hold values from 0 to 63
- deconv: float32 [256, 64], P('shot'), may hold values from -0.75 to 0.75
- focal_start: bfloat16 [8, 512, 256], P(None, 'rcv'), may hold values from -6 to 6
- onset_source: int32 [8, 256], P('rcv', 'shot'), may hold values from 32 to 128
- onset_receiver: int32 [8, 512], P('shot', 'rcv'), may hold values from 32 to 128
Outputs:
- upgoing_first: float32 [8, 256, 256], P('rcv', 'shot')
- downgoing: float32 [8, 512, 256], P('shot', 'rcv')
- upgoing_second: float32 [8, 256, 256], P('rcv', 'shot')
All inputs are finite; a program needn't handle non-finite values.
Results may differ from a plain program's by a relative error of at most 0.028.
Values may be sent and summed in bfloat16 or wider, within the bound.
No kernel may reach another device: no remote copies, remote signals or barrier semaphores. Data moves between devices by JAX's collectives and lax.ppermute only.
A program may use at most 64 MiB of HBM per device.

v0:
```python
import math
import jax
import jax.numpy as jnp
from jax import lax
from jax.sharding import PartitionSpec as P

NT = 256
NF = 128
TAPS = 64
KSHIFT = 64
exact_mode = lax.Precision.HIGHEST


def fourier_tables(length, bin_count):
    sample_ids = jnp.arange(length, dtype=jnp.int32)
    bin_ids = jnp.arange(bin_count, dtype=jnp.int32)
    phases = sample_ids[:, None] * bin_ids[None, :] % length
    angles = 2.0 * math.pi / length * phases.astype(jnp.float32)
    forward = jnp.concatenate([jnp.cos(angles), -jnp.sin(angles)], axis=1)
    weights = jnp.where(bin_ids == 0, 1.0, 2.0).astype(jnp.float32) / length
    inverse = jnp.concatenate(
        [jnp.cos(angles) * weights[None, :], -jnp.sin(angles) * weights[None, :]], axis=1
    ).T
    return (forward, inverse)


def delay_table(tap_count, kind_count):
    tap_index = jnp.arange(tap_count, dtype=jnp.float32)
    fraction = jnp.arange(kind_count, dtype=jnp.float32) * (tap_count / (4.0 * kind_count))
    offset = tap_index[None, :] - 0.375 * tap_count - fraction[:, None]
    window = 0.5 - 0.5 * jnp.cos(2.0 * math.pi * (tap_index + 0.5) / tap_count)
    return jnp.sinc(offset) * window[None, :]


def split_transform(signal, upper_part, lower_part, form):
    high_term = jnp.einsum(form, signal, upper_part, preferred_element_type=jnp.float32)
    low_term = jnp.einsum(form, signal, lower_part, preferred_element_type=jnp.float32)
    return high_term + low_term


def complex_product(left_op, right_op):
    real_part = left_op[0] * right_op[0] - left_op[1] * right_op[1]
    imag_part = left_op[0] * right_op[1] + left_op[1] * right_op[0]
    return jnp.stack([real_part, imag_part])


def apply_forward(matrix, focal_spec):

    def product_term(left_op, right_op):
        return jnp.einsum("fdau,fpd->fapu", left_op, right_op, preferred_element_type=jnp.float32)

    real_part = product_term(matrix[0], focal_spec[0]) - product_term(matrix[1], focal_spec[1])
    imag_part = product_term(matrix[0], focal_spec[1]) + product_term(matrix[1], focal_spec[0])
    return jnp.stack([real_part, imag_part])


def apply_adjoint(matrix, echo_spec):

    def product_term(left_op, right_op):
        return jnp.einsum("fdau,fapu->fpd", left_op, right_op, preferred_element_type=jnp.float32)

    real_part = product_term(matrix[0], echo_spec[0]) + product_term(matrix[1], echo_spec[1])
    imag_part = product_term(matrix[0], echo_spec[1]) - product_term(matrix[1], echo_spec[0])
    stacked = jnp.stack([real_part, imag_part])
    return stacked.reshape(
        stacked.shape[0], stacked.shape[1], stacked.shape[2], 1, stacked.shape[3]
    )


def to_time_field(spectra, onset, inverse):
    flat = spectra.reshape(-1, onset.shape[0], onset.shape[1])
    signal = jnp.einsum("cpu,ct->put", flat, inverse, precision=exact_mode)
    sample_ids = jnp.arange(inverse.shape[1], dtype=jnp.int32)
    folded = jnp.minimum(sample_ids, inverse.shape[1] - sample_ids)
    return jnp.where(folded[None, None, :] < onset[:, :, None], signal, 0.0)


def to_spectrum(signal, forward):
    flat = jnp.einsum("put,tc->cpu", signal, forward, precision=exact_mode)
    return flat.reshape(2, flat.shape[0] // 2, flat.shape[1], flat.shape[2])


def forward_sum(partial_value):
    return lax.psum_scatter(
        partial_value.astype(jnp.bfloat16), "rcv", scatter_dimension=3, tiled=True
    ).astype(jnp.float32)


def focal_rows(pieces):
    return lax.all_gather(pieces, "rcv", axis=3, tiled=True)


def time_layout(spectra):
    return lax.all_to_all(
        spectra.astype(jnp.bfloat16), "shot", split_axis=2, concat_axis=1, tiled=True
    ).astype(spectra.dtype)


def spectrum_layout(spectra):
    return lax.all_to_all(spectra, "shot", split_axis=1, concat_axis=2, tiled=True)


def body(traces, shift_index, deconv, focal_start, onset_source, onset_receiver):
    shot_count = lax.axis_size("shot")
    rcv_count = lax.axis_size("rcv")
    shot_index = lax.axis_index("shot")
    per_owner = NF // shot_count
    source_local = traces.shape[0]
    receiver_local = traces.shape[1]
    focal_total = focal_start.shape[0]
    focal_owned = focal_total // shot_count
    gain_factor = 1.0 / math.sqrt(NT * receiver_local * rcv_count)
    forward, inverse = fourier_tables(NT, NF)
    upper_part = forward.astype(jnp.bfloat16)
    lower_part = (forward - upper_part.astype(jnp.float32)).astype(jnp.bfloat16)
    tap_spec = jnp.dot(delay_table(TAPS, KSHIFT), forward[:TAPS], precision=exact_mode)
    wave_spec = jnp.dot(deconv, forward[:TAPS], precision=exact_mode)
    raw_spec = split_transform(traces, upper_part, lower_part, "srt,tc->crs").reshape(
        2, NF, receiver_local, source_local
    )
    kind_ids = jnp.arange(KSHIFT, dtype=jnp.int32)
    one_hot = (shift_index[:, :, None] == kind_ids[None, None, :]).astype(jnp.float32)
    delays = jnp.einsum("srm,mc->crs", one_hot, tap_spec, precision=exact_mode).reshape(
        2, NF, receiver_local, source_local
    )
    wavelet = wave_spec.T.reshape(2, NF, 1, source_local)
    reflection = (complex_product(complex_product(raw_spec, delays), wavelet) * gain_factor).astype(
        jnp.bfloat16
    )
    owned = lax.all_to_all(reflection, "shot", split_axis=1, concat_axis=3, tiled=True)
    matrix = owned.reshape(2, per_owner, receiver_local, shot_count, source_local)
    upper_band = lax.dynamic_slice_in_dim(
        upper_part.reshape(NT, 2, NF), shot_index * per_owner, per_owner, 2
    ).reshape(NT, 2 * per_owner)
    lower_band = lax.dynamic_slice_in_dim(
        lower_part.reshape(NT, 2, NF), shot_index * per_owner, per_owner, 2
    ).reshape(NT, 2 * per_owner)
    start_spec = split_transform(focal_start, upper_band, lower_band, "prt,tc->cpr").reshape(
        2, per_owner, focal_total, receiver_local
    )
    start_spec = start_spec.astype(jnp.bfloat16)
    summed = forward_sum(apply_forward(matrix, start_spec))
    summed = time_layout(summed)
    upgoing_first = to_time_field(summed, onset_source, inverse)
    echo_spec = to_spectrum(upgoing_first, forward).astype(jnp.bfloat16)
    echo_spec = echo_spec.reshape(2, NF, 1, echo_spec.shape[2], echo_spec.shape[3])
    echo_spec = spectrum_layout(echo_spec)
    echo_all = focal_rows(echo_spec)
    adjoint = apply_adjoint(matrix, echo_all)
    adjoint = time_layout(adjoint)
    focal_own = lax.dynamic_slice_in_dim(
        focal_start, shot_index * focal_owned, focal_owned, 0
    ).astype(jnp.float32)
    downgoing = focal_own + to_time_field(adjoint, onset_receiver, inverse)
    plus_spec = to_spectrum(downgoing, forward).astype(jnp.bfloat16)
    plus_spec = plus_spec.reshape(2, NF, focal_owned, 1, receiver_local)
    plus_spec = spectrum_layout(plus_spec)
    plus_spec = plus_spec.reshape(2, plus_spec.shape[1], focal_total, receiver_local)
    summed_again = forward_sum(apply_forward(matrix, plus_spec))
    summed_again = time_layout(summed_again)
    upgoing_second = to_time_field(summed_again, onset_source, inverse)
    return (upgoing_first, downgoing, upgoing_second)


def solution(mesh):
    placed = (
        P("shot", "rcv", None),
        P("shot", "rcv"),
        P("shot", None),
        P(None, "rcv", None),
        P("rcv", "shot"),
        P("shot", "rcv"),
    )
    return jax.shard_map(
        body,
        mesh=mesh,
        in_specs=placed,
        out_specs=(P("rcv", "shot", None), P("shot", "rcv", None), P("rcv", "shot", None)),
        check_vma=False,
    )
```

profile of v0, /device:TPU:0, one launch (start us, length us, event | category | flops | bytes accessed | tf_op | source)
XLA Modules:
  0.0 180.0 jit_solution(3745824398154742096)
XLA Ops:
  7.2 0.5 sine_negate_fusion
  7.8 1.0 copy-done
  8.8 0.7 fusion.38
  9.5 0.7 add_bitcast_fusion
  10.3 0.2 fusion.104
  10.6 0.3 convolution_bitcast_fusion.5
  10.9 1.8 %convolution_bitcast_fusion = f32[256,128,32]{1,0,2:T(8,128)S(1)} fusion(f32[64,256,1]{1,0,2:T(8,128)S(1)} %convolution_bitcast_fusion.5, s32[32,128]{1,0:T(8,128)S(1)} %copy-done.7), kind=kOutput, calls=%fused_computation.3 | convolution fusion | flops 805568512 | bytes 4276224 | tf_op jit(solution)/shard_map/srm,mc->crs/dot_general | solution.py:123
  12.8 1.5 subtract_bitcast_fusion
  14.3 1.3 add_bitcast_fusion.1
  15.6 0.6 fusion
  16.2 2.7 %copy.58 = bf16[2,128,128,32]{2,3,0,1:T(8,128)(2,1)} copy(bf16[2,128,128,32]{2,1,3,0:T(8,128)(2,1)S(1)} %fusion) | data formatting | bytes 4194304 | tf_op jit(solution)/shard_map/convert_element_type | solution.py:127
  18.8 5.3 %all-to-all-start = ((bf16[2,128,128,32]{2,3,0,1:T(8,128)(2,1)}), bf16[2,128,128,32]{2,3,0,1:T(8,128)(2,1)}, u32[]{:S(2)}, u32[]{:S(2)}) async-start(bf16[2,128,128,32]{2,3,0,1:T(8,128)(2,1)} %copy.58), calls=%async_computation | async-start | bytes 4194304 | tf_op jit(solution)/shard_map/all_to_all | solution.py:130
  24.1 0.2 reduce-scatter.3.cloned.1.call-start
  24.4 0.5 sine_negate_fusion.1
  25.0 0.2 fusion.126
  25.2 0.3 fusion.11
  25.5 25.4 %all-to-all-done = bf16[2,128,128,32]{2,3,0,1:T(8,128)(2,1)} async-done(((bf16[2,128,128,32]{2,3,0,1:T(8,128)(2,1)}), bf16[2,128,128,32]{2,3,0,1:T(8,128)(2,1)}, u32[]{:S(2)}, u32[]{:S(2)}) %all-to-all-start) | async-done | bytes 2097184 | tf_op jit(solution)/shard_map/all_to_all | solution.py:130
  50.9 2.2 %copy.136 = bf16[2,8,16,128,32]{3,4,1,2,0:T(8,128)(2,1)S(1)} copy(bf16[2,8,16,128,32]{3,4,0,2,1:T(8,128)(2,1)} %bitcast.12) | data formatting | bytes 4194304 | tf_op jit(solution)/shard_map/all_to_all | solution.py:130
  53.1 1.4 fusion.23
  54.6 1.5 fusion.22
  56.0 1.5 fusion.8
  57.5 1.5 fusion.7
  59.0 0.1 pad_maximum_fusion
  59.1 0.9 copy.65
  60.0 0.5 broadcast_multiply_fusion.1
  60.6 21.2 %reduce-scatter.3.cloned.1.call-done = bf16[2,16,8,2,32]{4,2,1,0,3:T(8,128)(2,1)} async-done(((bf16[2,16,8,8,32]{4,2,1,0,3:T(8,128)(2,1)}), bf16[2,16,8,2,32]{4,2,1,0,3:T(8,128)(2,1)}) %reduce-scatter.3.cloned.1.call-update) | async-done | bytes 32784 | tf_op jit(solution)/shard_map/reduce_scatter | solution.py:84
  81.8 1.0 copy.139
  82.8 0.8 reshape.232
  83.6 3.6 %all-to-all-start.1 = ((bf16[8,2,1024]{2,1,0:T(2,128)(2,1)}), bf16[8,2,1024]{2,1,0:T(2,128)(2,1)S(1)}, u32[]{:S(2)}, u32[]{:S(2)}) async-start(bf16[8,2,1024]{2,1,0:T(2,128)(2,1)} %reshape.232), calls=%async_computation.2 | async-start | bytes 65536 | tf_op jit(solution)/shard_map/all_to_all | solution.py:94
  87.2 4.8 %all-to-all-done.1 = bf16[8,2,1024]{2,1,0:T(2,128)(2,1)S(1)} async-done(((bf16[8,2,1024]{2,1,0:T(2,128)(2,1)}), bf16[8,2,1024]{2,1,0:T(2,128)(2,1)S(1)}, u32[]{:S(2)}, u32[]{:S(2)}) %all-to-all-start.1) | async-done | bytes 32800 | tf_op jit(solution)/shard_map/all_to_all | solution.py:94
  92.1 0.1 reshape.233
  92.2 0.1 bitcast_bitcast_fusion.1
  92.3 0.3 convolution_select_fusion.2
  92.6 0.4 convolution_convert_fusion.1
  93.0 0.1 copy.71
  93.2 0.2 reshape.234
  93.3 7.2 %all_to_all.93 = bf16[8,2,1024]{2,1,0:T(2,128)(2,1)S(1)} all-to-all(bf16[8,2,1024]{2,1,0:T(2,128)(2,1)S(1)} %reshape.234), channel_id=1, replica_groups=mesh['shot'=8,'rcv'=4] {'shot'}, dimensions={0} | all-to-all | bytes 65536 | tf_op jit(solution)/shard_map/all_to_all | solution.py:100
  100.6 0.1 reshape.235
  100.8 16.1 %all-gather = bf16[2,16,8,1,8,32]{5,2,3,1,0,4:T(8,128)(2,1)S(1)} all-gather(bf16[2,16,8,1,2,32]{5,2,3,1,0,4:T(8,128)(2,1)S(1)} %copy.73), channel_id=2, replica_groups=mesh['shot'=8,'rcv'=4] {'rcv'}, dimensions={4}, use_global_device_ids=true | all-gather | bytes 163840 | tf_op jit(solution)/shard_map/all_gather | solution.py:90
  116.9 0.5 convolution_bitcast_fusion.3
  117.4 0.5 convolution_bitcast_fusion.1
  117.9 0.5 fusion.17
  118.4 0.5 fusion.18
  118.9 0.6 copy.76
  119.5 3.4 %all-to-all-start.3 = ((bf16[2,16,8,1,128]{4,1,3,0,2:T(8,128)(2,1)}), bf16[2,16,8,1,128]{4,1,3,0,2:T(8,128)(2,1)S(1)}, u32[]{:S(2)}, u32[]{:S(2)}) async-start(bf16[2,16,8,1,128]{4,1,3,0,2:T(8,128)(2,1)} %copy.76), calls=%async_computation.4 | async-start | bytes 131072 | tf_op jit(solution)/shard_map/all_to_all | solution.py:94
  122.9 0.0 reduce-scatter.5.cloned.1.call-start
  123.0 4.9 %all-to-all-done.3 = bf16[2,16,8,1,128]{4,1,3,0,2:T(8,128)(2,1)S(1)} async-done(((bf16[2,16,8,1,128]{4,1,3,0,2:T(8,128)(2,1)}), bf16[2,16,8,1,128]{4,1,3,0,2:T(8,128)(2,1)S(1)}, u32[]{:S(2)}, u32[]{:S(2)}) %all-to-all-start.3) | async-done | bytes 65568 | tf_op jit(solution)/shard_map/all_to_all | solution.py:94
  127.9 0.3 fusion.10
  128.2 0.4 fusion.14
  128.5 0.1 copy.78
  128.6 7.4 %all_to_all.94 = bf16[2,128,1,1,128]{4,0,3,2,1:T(2,128)(2,1)S(1)} all-to-all(bf16[2,128,1,1,128]{4,0,3,2,1:T(2,128)(2,1)S(1)} %copy.78), channel_id=1, replica_groups=mesh['shot'=8,'rcv'=4] {'shot'}, dimensions={1} | all-to-all | bytes 131072 | tf_op jit(solution)/shard_map/all_to_all | solution.py:100
  136.1 2.7 %fusion.21 = f32[16,8,8,32]{3,1,2,0:T(8,128)S(1)} fusion(bf16[2,16,128,8,32]{2,4,3,1,0:T(8,128)(2,1)} %bitcast.192, bf16[2,16,8,1,1,128]{5,2,1,4,3,0:T(8,128)(2,1)S(1)} %bitcast.201), kind=kOutput, calls=%fused_computation.49 | convolution fusion | flops 8388608 | bytes 1212416 | tf_op jit(solution)/shard_map/fdau,fpd->fapu/dot_general | solution.py:50
  138.7 1.5 fusion.20
  140.2 1.5 fusion.6
  141.7 1.5 fusion.5
  143.1 0.1 pad_maximum_fusion.1
  143.3 0.9 copy.81
  144.2 18.3 %reduce-scatter.5.cloned.1.call-done = bf16[2,16,8,2,32]{4,2,1,0,3:T(8,128)(2,1)} async-done(((bf16[2,16,8,8,32]{4,2,1,0,3:T(8,128)(2,1)}), bf16[2,16,8,2,32]{4,2,1,0,3:T(8,128)(2,1)}) %reduce-scatter.5.cloned.1.call-update) | async-done | bytes 32784 | tf_op jit(solution)/shard_map/reduce_scatter | solution.py:84
  162.5 1.0 copy.138
  163.6 0.2 reshape.236
  163.7 8.3 %all_to_all.95 = bf16[8,2,1024]{2,1,0:T(2,128)(2,1)S(1)} all-to-all(bf16[8,2,1024]{2,1,0:T(2,128)(2,1)S(1)} %reshape.236), channel_id=1, replica_groups=mesh['shot'=8,'rcv'=4] {'shot'}, dimensions={0} | all-to-all | bytes 65536 | tf_op jit(solution)/shard_map/all_to_all | solution.py:94
  172.0 0.1 reshape.237
  172.2 0.1 bitcast_bitcast_fusion
  172.3 0.9 convolution_select_fusion.1
  (42 shorter events, 0.4 us)
Async XLA Ops:
  7.2 1.6 copy-start
  9.5 0.8 copy-start.8
  9.5 1.4 copy-start.7
  18.8 6.1 %copy-start.4 = (bf16[8,128,256]{2,1,0:T(8,128)(2,1)S(1)}, bf16[8,128,256]{2,1,0:T(8,128)(2,1)}, u32[]{:S(2)}) copy-start(bf16[8,128,256]{2,1,0:T(8,128)(2,1)} %param.9) | copy-start | bytes 1572868
  18.8 32.1 %all-to-all-start = ((bf16[2,128,128,32]{2,3,0,1:T(8,128)(2,1)}), bf16[2,128,128,32]{2,3,0,1:T(8,128)(2,1)}, u32[]{:S(2)}, u32[]{:S(2)}) async-start(bf16[2,128,128,32]{2,3,0,1:T(8,128)(2,1)} %copy.58), calls=%async_computation | async-start | bytes 4194304 | tf_op jit(solution)/shard_map/all_to_all | solution.py:130
  24.1 57.6 %reduce-scatter.3.cloned.1.call-start = ((), (), s32[]{:S(2)}) async-start(), calls=%async_computation.8 | async-start | bytes 655360 | tf_op jit(solution)/shard_map/reduce_scatter | solution.py:84
  53.1 4.4 %copy-start.1 = (bf16[2,8,16,128,32]{3,4,1,2,0:T(8,128)(2,1)}, bf16[2,8,16,128,32]{3,4,1,2,0:T(8,128)(2,1)S(1)}, u32[]{:S(2)}) copy-start(bf16[2,8,16,128,32]{3,4,1,2,0:T(8,128)(2,1)S(1)} %copy.136) | copy-start | bytes 6291460
  59.0 33.4 %copy-start.9 = (s32[2,32]{1,0:T(2,128)S(1)}, s32[2,32]{1,0:T(2,128)}, u32[]{:S(2)}) copy-start(s32[2,32]{1,0:T(2,128)} %param.10) | copy-start | bytes 772
  83.6 8.5 %all-to-all-start.1 = ((bf16[8,2,1024]{2,1,0:T(2,128)(2,1)}), bf16[8,2,1024]{2,1,0:T(2,128)(2,1)S(1)}, u32[]{:S(2)}, u32[]{:S(2)}) async-start(bf16[8,2,1024]{2,1,0:T(2,128)(2,1)} %reshape.232), calls=%async_computation.2 | async-start | bytes 65536 | tf_op jit(solution)/shard_map/all_to_all | solution.py:94
  92.6 24.8 %copy-start.6 = (f32[2,32,256]{2,1,0:T(8,128)}, f32[2,32,256]{2,1,0:T(8,128)S(1)}, u32[]{:S(2)}) copy-start(f32[2,32,256]{2,1,0:T(8,128)S(1)} %convolution_select_fusion.2) | copy-start | bytes 196612
  100.7 16.2 %copy-start.2 = (bf16[2,8,16,128,32]{3,4,1,2,0:T(8,128)(2,1)S(1)}, bf16[2,8,16,128,32]{3,4,1,2,0:T(8,128)(2,1)}, u32[]{:S(2)}) copy-start(bf16[2,8,16,128,32]{3,4,1,2,0:T(8,128)(2,1)} %copy-done.1) | copy-start | bytes 6291460
  117.9 10.0 %copy-start.10 = (s32[1,128]{1,0:T(1,128)S(1)}, s32[1,128]{1,0:T(1,128)}, u32[]{:S(2)}) copy-start(s32[1,128]{1,0:T(1,128)} %param.11) | copy-start | bytes 1540
  119.5 8.3 %all-to-all-start.3 = ((bf16[2,16,8,1,128]{4,1,3,0,2:T(8,128)(2,1)}), bf16[2,16,8,1,128]{4,1,3,0,2:T(8,128)(2,1)S(1)}, u32[]{:S(2)}, u32[]{:S(2)}) async-start(bf16[2,16,8,1,128]{4,1,3,0,2:T(8,128)(2,1)} %copy.76), calls=%async_computation.4 | async-start | bytes 131072 | tf_op jit(solution)/shard_map/all_to_all | solution.py:94
  122.9 39.6 %reduce-scatter.5.cloned.1.call-start = ((), (), s32[]{:S(2)}) async-start(), calls=%async_computation.9 | async-start | bytes 655360 | tf_op jit(solution)/shard_map/reduce_scatter | solution.py:84
  127.8 10.9 %copy-start.3 = (bf16[2,8,16,128,32]{3,4,1,2,0:T(8,128)(2,1)S(1)}, bf16[2,8,16,128,32]{3,4,1,2,0:T(8,128)(2,1)}, u32[]{:S(2)}) copy-start(bf16[2,8,16,128,32]{3,4,1,2,0:T(8,128)(2,1)} %copy-done.1) | copy-start | bytes 6291460
  128.1 13.5 %copy-start.5 = (f32[1,128,256]{2,1,0:T(8,128)}, f32[1,128,256]{2,1,0:T(8,128)S(1)}, u32[]{:S(2)}) copy-start(f32[1,128,256]{2,1,0:T(8,128)S(1)} %fusion.10) | copy-start | bytes 393220
Sparse Core Ops, SparseCore 0:
  60.2 21.5 reduce-scatter.2
  144.3 18.1 reduce-scatter.4
where the time goes:
time: 181 us; the launch traced here: 180 us
  waiting for transfers between devices  74.6 us (41%)
  blocking collectives  39 us (22%)
  matrix products  21.5 us (12%)
  between operations  14.5 us (8%)
  starting transfers between devices  12.6 us (7%)
  local copies, waits for them, and re-layouts  12.5 us (7%)
  other arithmetic  5.39 us (3%)
    reduce_scatter x2, waiting for transfers between devices, forward_sum(): lax.psum_scatter(partial_value.astype(jnp.bfloat16), 'rcv', scatter_dimen...  39.5 us
    all_to_all x1, waiting for transfers between devices, body(): lax.all_to_all(reflection, 'shot', split_axis=1, concat_axis=3, tiled=True)  25.4 us
    all_gather x1, blocking collectives, focal_rows(): return lax.all_gather(pieces, 'rcv', axis=3, tiled=True)  16.1 us
    all_to_all x2, blocking collectives, spectrum_layout(): lax.all_to_all(spectra, 'shot', split_axis=1, concat_axis=2, tiled=True)  14.6 us
    dot_general x8, matrix products, product_term(): jnp.einsum('fdau,fpd->fapu', left_op, right_op, preferred_element_type=jn...  12.9 us
    all_to_all x2, waiting for transfers between devices, time_layout(): lax.all_to_all(spectra.astype(jnp.bfloat16), 'shot', split_axis=2, concat...  9.71 us
    all_to_all x1, blocking collectives, time_layout(): lax.all_to_all(spectra.astype(jnp.bfloat16), 'shot', split_axis=2, concat...  8.29 us
    all_to_all x2, starting transfers between devices, time_layout(): lax.all_to_all(spectra.astype(jnp.bfloat16), 'shot', split_axis=2, concat...  6.99 us
  transfers between devices with their start and end apart: 5, of which 5 were waited for; matrix products, arithmetic and copies ran while one was open for 1% of the time, Pallas kernels for 0%

commit v1 on v0

--- a/solution.py
+++ b/solution.py
@@ -1,14 +1,31 @@
+import functools
 import math
 import jax
 import jax.numpy as jnp
 from jax import lax
 from jax.sharding import PartitionSpec as P
+from jax.lax import all_to_all, axis_size
 
 NT = 256
 NF = 128
 TAPS = 64
 KSHIFT = 64
 exact_mode = lax.Precision.HIGHEST
+
+
+def _return_all_roots(shard_in, axis_name, row_dim, ndim_at):
+    return jnp.concatenate(
+        all_to_all(
+            jnp.stack(jnp.split(shard_in, axis_size(axis_name), axis=row_dim), axis=0),
+            axis_name,
+            0,
+            0,
+        ),
+        axis=ndim_at,
+    )
+
+
+_see_scenes = functools.partial(_return_all_roots, axis_name="shot", row_dim=1, ndim_at=3)
 
 
 def fourier_tables(length, bin_count):
@@ -127,7 +144,7 @@
     reflection = (complex_product(complex_product(raw_spec, delays), wavelet) * gain_factor).astype(
         jnp.bfloat16
     )
-    owned = lax.all_to_all(reflection, "shot", split_axis=1, concat_axis=3, tiled=True)
+    owned = _see_scenes(reflection)
     matrix = owned.reshape(2, per_owner, receiver_local, shot_count, source_local)
     upper_band = lax.dynamic_slice_in_dim(
         upper_part.reshape(NT, 2, NF), shot_index * per_owner, per_owner, 2

time: 181 us -> 202 us (1.12)
  local copies, waits for them, and re-layouts: 12.5 us -> 27.7 us
  matrix products: 21.5 us -> 25.3 us
    unnamed x28 -> x37, local copies, waits for them, and re-layouts: 2.55 us -> 13.8 us
    convert_element_type x2, local copies, waits for them, and re-layouts: 0.15 us -> 2.94 us  [body(): echo_spec = to_spectrum(upgoing_first, forward).astype(jnp.bfloat16)]
    convert_element_type x1 -> x0, local copies, waits for them, and re-layouts: 2.66 us -> none  [body(): (complex_product(complex_product(raw_spec, delays), wavelet) * gain_facto...]
    all_to_all x1 -> x0, local copies, waits for them, and re-layouts: 2.21 us -> none  [body(): lax.all_to_all(reflection, 'shot', split_axis=1, concat_axis=3, tiled=True)]
  transfers between devices with their start and end apart: 5 -> 5, of which waited for: 5 -> 5; matrix products, arithmetic and copies ran while one was open for 1% -> 2% of each run, Pallas kernels for 0% -> 0%
where the time goes in v1:
time: 202 us; the launch traced here: 201 us
  waiting for transfers between devices  73.3 us (36%)
  blocking collectives  40.4 us (20%)
  local copies, waits for them, and re-layouts  27.7 us (14%)
  matrix products  25.3 us (13%)
  between operations  14.4 us (7%)
  starting transfers between devices  13.5 us (7%)
  other arithmetic  6.73 us (3%)
    reduce_scatter x2, waiting for transfers between devices, forward_sum(): lax.psum_scatter(partial_value.astype(jnp.bfloat16), 'rcv', scatter_dimen...  38.8 us
    all_to_all x1, waiting for transfers between devices, _return_all_roots(): all_to_all(jnp.stack(jnp.split(shard_in, axis_size(axis_name), axis=row_d...  25.4 us
    all_to_all x2, blocking collectives, spectrum_layout(): lax.all_to_all(spectra, 'shot', split_axis=1, concat_axis=2, tiled=True)  16.2 us
    all_gather x1, blocking collectives, focal_rows(): return lax.all_gather(pieces, 'rcv', axis=3, tiled=True)  15.9 us
    unnamed x37, local copies, waits for them, and re-layouts  13.8 us
    dot_general x8, matrix products, product_term(): jnp.einsum('fdau,fpd->fapu', left_op, right_op, preferred_element_type=jn...  13 us
    all_to_all x2, waiting for transfers between devices, time_layout(): lax.all_to_all(spectra.astype(jnp.bfloat16), 'shot', split_axis=2, concat...  9.1 us
    all_to_all x1, blocking collectives, time_layout(): lax.all_to_all(spectra.astype(jnp.bfloat16), 'shot', split_axis=2, concat...  8.26 us
  transfers between devices with their start and end apart: 5, of which 5 were waited for; matrix products, arithmetic and copies ran while one was open for 2% of the time, Pallas kernels for 0%

profile of v1, /device:TPU:0, one launch (start us, length us, event | category | flops | bytes accessed | tf_op | source)
XLA Modules:
  0.0 201.3 jit_solution(16214297581110870226)
XLA Ops:
  7.2 0.5 sine_negate_fusion
  7.8 1.0 copy-done
  8.8 0.7 fusion.58
  9.5 0.7 add_bitcast_fusion
  10.9 1.8 convolution_bitcast_fusion
  12.7 1.5 subtract_bitcast_fusion
  14.3 1.3 add_bitcast_fusion.1
  15.6 0.6 fusion
  16.2 0.7 fusion.44
  16.9 0.7 fusion.43
  17.6 0.8 fusion.42
  18.4 0.7 fusion.41
  19.1 0.8 fusion.40
  19.9 0.7 fusion.39
  20.6 0.7 fusion.38
  21.4 0.7 fusion.37
  22.1 5.3 %all-to-all-start = ((bf16[8,2,16,128,32]{3,2,4,1,0:T(8,128)(2,1)}), bf16[8,2,16,128,32]{3,2,4,1,0:T(8,128)(2,1)}, u32[]{:S(2)}, u32[]{:S(2)}) async-start(bf16[8,2,16,128,32]{3,2,4,1,0:T(8,128)(2,1)} %fusion.37), calls=%async_computation | async-start | bytes 4194304 | tf_op jit(solution)/shard_map/all_to_all | solution.py:18
  27.7 0.5 sine_negate_fusion.1
  28.8 25.4 %all-to-all-done = bf16[8,2,16,128,32]{3,2,4,1,0:T(8,128)(2,1)} async-done(((bf16[8,2,16,128,32]{3,2,4,1,0:T(8,128)(2,1)}), bf16[8,2,16,128,32]{3,2,4,1,0:T(8,128)(2,1)}, u32[]{:S(2)}, u32[]{:S(2)}) %all-to-all-start) | async-done | bytes 2097184 | tf_op jit(solution)/shard_map/all_to_all | solution.py:18
  54.2 1.9 slice_bitcast_fusion
  56.1 1.5 fusion.34
  57.6 1.5 fusion.32
  59.0 1.5 fusion.8
  60.5 1.5 fusion.7
  62.1 0.9 copy.99
  63.1 1.2 broadcast_multiply_fusion.1
  64.3 20.5 %reduce-scatter.3.cloned.1.call-done = bf16[2,16,8,2,32]{4,2,1,0,3:T(8,128)(2,1)} async-done(((bf16[2,16,8,8,32]{4,2,1,0,3:T(8,128)(2,1)}), bf16[2,16,8,2,32]{4,2,1,0,3:T(8,128)(2,1)}) %reduce-scatter.3.cloned.1.call-update) | async-done | bytes 32784 | tf_op jit(solution)/shard_map/reduce_scatter | solution.py:101
  84.8 1.7 copy.201
  86.5 1.7 reshape.232
  88.2 4.0 %all-to-all-start.1 = ((bf16[8,2,1024]{2,1,0:T(2,128)(2,1)}), bf16[8,2,1024]{2,1,0:T(2,128)(2,1)}, u32[]{:S(2)}, u32[]{:S(2)}) async-start(bf16[8,2,1024]{2,1,0:T(2,128)(2,1)} %reshape.232), calls=%async_computation.2 | async-start | bytes 65536 | tf_op jit(solution)/shard_map/all_to_all | solution.py:111
  92.1 4.8 %all-to-all-done.1 = bf16[8,2,1024]{2,1,0:T(2,128)(2,1)} async-done(((bf16[8,2,1024]{2,1,0:T(2,128)(2,1)}), bf16[8,2,1024]{2,1,0:T(2,128)(2,1)}, u32[]{:S(2)}, u32[]{:S(2)}) %all-to-all-start.1) | async-done | bytes 32800 | tf_op jit(solution)/shard_map/all_to_all | solution.py:111
  97.0 1.6 reshape.233
  98.5 1.0 bitcast_bitcast_fusion.1
  99.6 1.2 convolution_select_fusion.2
  100.8 0.6 copy-done.7
  101.4 1.0 convolution_convert_fusion.1
  102.4 1.4 convert_element_type.103
  103.8 1.6 copy.105
  105.3 1.7 reshape.234
  107.0 8.8 %all_to_all.83 = bf16[8,2,1024]{2,1,0:T(2,128)(2,1)} all-to-all(bf16[8,2,1024]{2,1,0:T(2,128)(2,1)} %reshape.234), channel_id=1, replica_groups=mesh['shot'=8,'rcv'=4] {'shot'}, dimensions={0} | all-to-all | bytes 65536 | tf_op jit(solution)/shard_map/all_to_all | solution.py:117
  115.8 1.6 reshape.235
  117.4 0.9 copy.106
  118.3 15.9 %all-gather = bf16[2,16,8,1,8,32]{5,2,3,1,0,4:T(8,128)(2,1)S(1)} all-gather(bf16[2,16,8,1,2,32]{5,2,3,1,0,4:T(8,128)(2,1)S(1)} %copy.107), channel_id=2, replica_groups=mesh['shot'=8,'rcv'=4] {'rcv'}, dimensions={4}, use_global_device_ids=true | all-gather | bytes 163840 | tf_op jit(solution)/shard_map/all_gather | solution.py:107
  134.3 0.5 convolution_bitcast_fusion.3
  134.9 0.5 convolution_bitcast_fusion.1
  135.5 0.6 fusion.17
  136.1 0.6 fusion.18
  136.7 0.6 copy.114
  137.3 4.0 %all-to-all-start.3 = ((bf16[2,16,8,1,128]{4,1,3,0,2:T(8,128)(2,1)}), bf16[2,16,8,1,128]{4,1,3,0,2:T(8,128)(2,1)}, u32[]{:S(2)}, u32[]{:S(2)}) async-start(bf16[2,16,8,1,128]{4,1,3,0,2:T(8,128)(2,1)} %copy.114), calls=%async_computation.4 | async-start | bytes 131072 | tf_op jit(solution)/shard_map/all_to_all | solution.py:111
  141.3 0.7 pad_maximum_fusion.3
  142.0 4.3 %all-to-all-done.3 = bf16[2,16,8,1,128]{4,1,3,0,2:T(8,128)(2,1)} async-done(((bf16[2,16,8,1,128]{4,1,3,0,2:T(8,128)(2,1)}), bf16[2,16,8,1,128]{4,1,3,0,2:T(8,128)(2,1)}, u32[]{:S(2)}, u32[]{:S(2)}) %all-to-all-start.3) | async-done | bytes 65568 | tf_op jit(solution)/shard_map/all_to_all | solution.py:111
  146.3 0.9 copy.115
  147.2 1.2 fusion.10
  148.4 1.4 fusion.14
  149.9 7.4 %all_to_all.84 = bf16[2,128,1,1,128]{4,0,3,2,1:T(2,128)(2,1)S(1)} all-to-all(bf16[2,128,1,1,128]{4,0,3,2,1:T(2,128)(2,1)S(1)} %copy.116), channel_id=1, replica_groups=mesh['shot'=8,'rcv'=4] {'shot'}, dimensions={1} | all-to-all | bytes 131072 | tf_op jit(solution)/shard_map/all_to_all | solution.py:117
  157.3 2.7 %fusion.28 = f32[16,8,8,32]{3,1,2,0:T(8,128)S(1)} fusion(bf16[16,128,8,32]{1,0,3,2:T(8,128)(2,1)} %copy-done.1, bf16[2,16,8,1,1,128]{5,2,1,4,3,0:T(8,128)(2,1)S(1)} %bitcast.206), kind=kOutput, calls=%fused_computation.55 | convolution fusion | flops 8388608 | bytes 1212416 | tf_op jit(solution)/shard_map/fdau,fpd->fapu/dot_general | solution.py:67
  160.0 1.5 fusion.26
  161.5 1.5 fusion.6
  163.0 1.5 fusion.5
  164.6 0.9 copy.123
  165.5 18.3 %reduce-scatter.5.cloned.1.call-done = bf16[2,16,8,2,32]{4,2,1,0,3:T(8,128)(2,1)} async-done(((bf16[2,16,8,8,32]{4,2,1,0,3:T(8,128)(2,1)}), bf16[2,16,8,2,32]{4,2,1,0,3:T(8,128)(2,1)}) %reduce-scatter.5.cloned.1.call-update) | async-done | bytes 32784 | tf_op jit(solution)/shard_map/reduce_scatter | solution.py:101
  183.8 1.0 copy.200
  185.0 8.3 %all_to_all.85 = bf16[8,2,1024]{2,1,0:T(2,128)(2,1)S(1)} all-to-all(bf16[8,2,1024]{2,1,0:T(2,128)(2,1)S(1)} %reshape.236), channel_id=1, replica_groups=mesh['shot'=8,'rcv'=4] {'shot'}, dimensions={0} | all-to-all | bytes 65536 | tf_op jit(solution)/shard_map/all_to_all | solution.py:111
  193.6 0.9 convolution_select_fusion.1
  (51 shorter events, 2.5 us)
Async XLA Ops:
  7.2 1.6 copy-start
  9.5 0.8 copy-start.9
  9.5 1.4 copy-start.8
  22.1 6.2 %copy-start.4 = (bf16[8,128,256]{2,1,0:T(8,128)(2,1)S(1)}, bf16[8,128,256]{2,1,0:T(8,128)(2,1)}, u32[]{:S(2)}) copy-start(bf16[8,128,256]{2,1,0:T(8,128)(2,1)} %param.9) | copy-start | bytes 1572868
  22.1 32.1 %all-to-all-start = ((bf16[8,2,16,128,32]{3,2,4,1,0:T(8,128)(2,1)}), bf16[8,2,16,128,32]{3,2,4,1,0:T(8,128)(2,1)}, u32[]{:S(2)}, u32[]{:S(2)}) async-start(bf16[8,2,16,128,32]{3,2,4,1,0:T(8,128)(2,1)} %fusion.37), calls=%async_computation | async-start | bytes 4194304 | tf_op jit(solution)/shard_map/all_to_all | solution.py:18
  27.4 57.4 %reduce-scatter.3.cloned.1.call-start = ((), (), s32[]{:S(2)}) async-start(), calls=%async_computation.8 | async-start | bytes 655360 | tf_op jit(solution)/shard_map/reduce_scatter | solution.py:101
  56.1 4.4 %copy-start.1 = (bf16[16,128,8,32]{1,0,3,2:T(8,128)(2,1)}, bf16[16,128,8,32]{1,0,3,2:T(8,128)(2,1)S(1)}, u32[]{:S(2)}) copy-start(bf16[16,128,8,32]{1,0,3,2:T(8,128)(2,1)S(1)} %get-tuple-element.7) | copy-start | bytes 3145732
  62.0 37.6 %copy-start.10 = (s32[2,32]{1,0:T(2,128)S(1)}, s32[2,32]{1,0:T(2,128)}, u32[]{:S(2)}) copy-start(s32[2,32]{1,0:T(2,128)} %param.10) | copy-start | bytes 772
  88.2 8.8 %all-to-all-start.1 = ((bf16[8,2,1024]{2,1,0:T(2,128)(2,1)}), bf16[8,2,1024]{2,1,0:T(2,128)(2,1)}, u32[]{:S(2)}, u32[]{:S(2)}) async-start(bf16[8,2,1024]{2,1,0:T(2,128)(2,1)} %reshape.232), calls=%async_computation.2 | async-start | bytes 65536 | tf_op jit(solution)/shard_map/all_to_all | solution.py:111
  100.8 0.6 copy-start.7
  134.3 1.2 copy-start.2
  135.5 11.7 %copy-start.11 = (s32[1,128]{1,0:T(1,128)S(1)}, s32[1,128]{1,0:T(1,128)}, u32[]{:S(2)}) copy-start(s32[1,128]{1,0:T(1,128)} %param.11) | copy-start | bytes 1540
  137.3 9.0 %all-to-all-start.3 = ((bf16[2,16,8,1,128]{4,1,3,0,2:T(8,128)(2,1)}), bf16[2,16,8,1,128]{4,1,3,0,2:T(8,128)(2,1)}, u32[]{:S(2)}, u32[]{:S(2)}) async-start(bf16[2,16,8,1,128]{4,1,3,0,2:T(8,128)(2,1)} %copy.114), calls=%async_computation.4 | async-start | bytes 131072 | tf_op jit(solution)/shard_map/all_to_all | solution.py:111
  141.3 42.6 %reduce-scatter.5.cloned.1.call-start = ((), (), s32[]{:S(2)}) async-start(), calls=%async_computation.9 | async-start | bytes 655360 | tf_op jit(solution)/shard_map/reduce_scatter | solution.py:101
  146.3 13.7 %copy-start.3 = (bf16[16,128,8,32]{1,0,3,2:T(8,128)(2,1)S(1)}, bf16[16,128,8,32]{1,0,3,2:T(8,128)(2,1)}, u32[]{:S(2)}) copy-start(bf16[16,128,8,32]{1,0,3,2:T(8,128)(2,1)} %copy-done.1) | copy-start | bytes 3145732
  148.4 8.9 %copy-start.6 = (f32[1,128,256]{2,1,0:T(8,128)}, f32[1,128,256]{2,1,0:T(8,128)S(1)}, u32[]{:S(2)}) copy-start(f32[1,128,256]{2,1,0:T(8,128)S(1)} %fusion.10) | copy-start | bytes 393220
  164.4 29.1 %copy-start.5 = (f32[256,128]{0,1:T(8,128)S(1)}, f32[256,128]{0,1:T(8,128)}, u32[]{:S(2)}) copy-start(f32[256,128]{0,1:T(8,128)} %get-tuple-element.15) | copy-start | bytes 393220
Sparse Core Ops, SparseCore 0:
  63.2 21.5 reduce-scatter.2
  165.6 18.1 reduce-scatter.4
